TPU v7x, 128 devices: a whole 4x4x4 slice. The times are simulated.
128 devices in a mesh: tensor: 4 (over x), feat: 32 (over y, z, core).
Axes of the slice: x: 4, y: 4, z: 4, core: 2. Of those that a mesh axis runs over, the one named last changes fastest.
Arguments:
- feat_ids: int32 [512, 32], P('feat'), may hold values from 0 to 131071, as said below
- feat_acts: float32 [512, 32], P('feat'), may hold values from 0.1 to 3
- target_ids: int32 [1024], replicated, may hold values from 0 to 131071
- target_token_positions: int32 [1024], replicated, may hold values from 0 to 511
- encoder: bfloat16 [131072, 4608], P('feat', 'tensor'), may hold values from -0.59765625 to 0.59765625
- decoder: bfloat16 [131072, 4608], P('feat', 'tensor'), may hold values from -0.59765625 to 0.59765625
- queries: bfloat16 [512, 2048], P('feat', 'tensor'), may hold values from -6 to 6
- keys: bfloat16 [512, 1024], P('feat', 'tensor'), may hold values from -6 to 6
- w_out: bfloat16 [2048, 4608], P(None, 'tensor'), may hold values from -1.1953125 to 1.1953125
- w_value: bfloat16 [4608, 1024], P('tensor'), may hold values from -1.1953125 to 1.1953125
- ln_gain: float32 [4608], P('tensor'), may hold values from 0.3 to 3
- norm_scale: float32 [512], P('feat'), may hold values from 0.3 to 3
Outputs:
- edges: float32 [512, 32, 1024], P('feat', None, 'tensor')
Inputs may be any that keep to these rules, and one draw needn't show every extreme that they name: `feat_ids`: split the ids into aligned blocks of 512 entries (the tokens of one device, in order) and the ids into feature blocks of 4096 (id // 4096): no feature block holds more than 64 entries of one token block, and one feature block holds exactly 64 entries of every token block.
All inputs are finite; a program needn't handle non-finite values.
Results may differ from a plain program's by a relative error of at most 0.0085.
Values may be sent and summed in bfloat16 or wider, within the bound.
A program may use at most 128 MiB of HBM per device.

v0:
```python
import jax
import jax.numpy as jnp
from jax import lax
from jax.sharding import PartitionSpec as P

HD = 128
H = 16
KVH = 8


softcap_value = 50.0
query_scale = 144.0 ** (-0.5)


def side_by_side(arrays, axis, dim, along):
    both = jnp.concatenate(arrays, axis=along)
    out, at, outs = (lax.all_gather(both, axis, axis=dim, tiled=True), 0, [])
    for a in arrays:
        outs.append(lax.slice_in_dim(out, at, at + a.shape[along], axis=along))
        at += a.shape[along]
    return tuple(outs)


def per_device(
    feat_ids,
    feat_acts,
    target_ids,
    target_token_positions,
    encoder,
    decoder,
    queries,
    keys,
    w_out,
    w_value,
    ln_gain,
    norm_scale,
):
    feat_count = lax.axis_size("feat")
    feat_index = lax.axis_index("feat")
    feat_dev = encoder.shape[0]
    tok_dev, active = feat_ids.shape
    targets = target_ids.shape[0]
    groups = H // KVH
    local_kv = keys.shape[1] // HD
    all_queries, all_keys = side_by_side((queries, keys), "feat", 0, 1)
    query_rows = all_queries[target_token_positions]
    target_owner = target_ids // feat_dev
    target_row = target_ids - target_owner * feat_dev
    is_owner = (target_owner == feat_index)[:, None]
    seed_part = jnp.where(is_owner, encoder[target_row].astype(jnp.float32), jnp.float32(0.0))
    seed_row_block = lax.psum(seed_part.astype(jnp.bfloat16), "feat")
    w_piece = w_out
    back_local = lax.psum_scatter(
        lax.dot_general(
            w_piece, seed_row_block, (((1,), (1,)), ((), ())), preferred_element_type=jnp.float32
        ),
        "tensor",
        scatter_dimension=0,
        tiled=True,
    )
    back_heads = lax.optimization_barrier(back_local.astype(jnp.bfloat16)).astype(jnp.float32)
    back_heads = back_heads.reshape(local_kv, groups, HD, targets)
    query_head_count = query_rows.reshape(targets, local_kv, groups, HD)
    positions = feat_index * tok_dev + jnp.arange(tok_dev, dtype=jnp.int32)
    scores = (
        jnp.einsum(
            "bkge,tke->bkgt",
            query_head_count,
            all_keys.reshape(-1, local_kv, HD),
            preferred_element_type=jnp.float32,
        )
        * query_scale
    )
    capped = softcap_value * jnp.tanh(scores / softcap_value)
    causal = (
        jnp.arange(all_keys.shape[0], dtype=jnp.int32)[None, :] <= target_token_positions[:, None]
    )
    everywhere = jnp.where(causal[:, None, None, :], jnp.exp(capped), jnp.float32(0.0))
    denominator_sum = jnp.sum(everywhere, axis=3)
    weights = lax.dynamic_slice_in_dim(everywhere, feat_index * tok_dev, tok_dev, 3)
    pattern = weights / denominator_sum[..., None]
    value_grad = jnp.einsum("bkgt,kgeb->tbke", pattern, back_heads)
    value_grad = value_grad.reshape(tok_dev, targets, local_kv * HD).astype(jnp.bfloat16)
    flat_ids = feat_ids.reshape(-1)
    row_total = flat_ids.shape[0]
    capacity = max(2, row_total // 8, -(-row_total // feat_count))
    owner_id = flat_ids // feat_dev
    local_row = flat_ids - owner_id * feat_dev
    onehot = (owner_id[:, None] == jnp.arange(feat_count, dtype=jnp.int32)[None, :]).astype(
        jnp.int32
    )
    slot_index = jnp.sum((jnp.cumsum(onehot, axis=0) - onehot) * onehot, axis=1)
    request_table = (
        jnp.full((feat_count, capacity), -1, jnp.int32).at[owner_id, slot_index].set(local_row)
    )
    wanted = lax.all_to_all(request_table, "feat", split_axis=0, concat_axis=0, tiled=True)
    found_rows = jnp.where(
        (wanted >= 0)[..., None], decoder[jnp.maximum(wanted, 0)], jnp.zeros((), jnp.bfloat16)
    )
    returned = lax.all_to_all(found_rows, "feat", split_axis=0, concat_axis=0, tiled=True)
    fetched = returned[owner_id, slot_index]
    gained = (fetched.astype(jnp.float32) * ln_gain).astype(jnp.bfloat16)
    w_piece = w_value
    projected = lax.psum_scatter(
        lax.dot_general(
            w_piece, gained, (((0,), (1,)), ((), ())), preferred_element_type=jnp.float32
        ),
        "tensor",
        scatter_dimension=0,
        tiled=True,
    )
    projected = projected.astype(jnp.bfloat16).reshape(-1, tok_dev, active)
    attention = jnp.einsum(
        "jtk,tbj->tkb", projected, value_grad, preferred_element_type=jnp.float32
    )
    direct = lax.dot_general(
        fetched, seed_row_block, (((1,), (1,)), ((), ())), preferred_element_type=jnp.float32
    )
    direct = direct.reshape(tok_dev, active, targets)
    at_target = (positions[:, None] == target_token_positions[None, :])[:, None, :]
    direct = jnp.where(at_target, direct, jnp.float32(0.0))
    edge_term = feat_acts[:, :, None] * (direct + norm_scale[:, None, None] * attention)
    return lax.psum_scatter(edge_term, "tensor", scatter_dimension=2, tiled=True)


def solution(mesh):
    in_specs = (
        P("feat", None),
        P("feat", None),
        P(),
        P(),
        P("feat", "tensor"),
        P("feat", "tensor"),
        P("feat", "tensor"),
        P("feat", "tensor"),
        P(None, "tensor"),
        P("tensor", None),
        P("tensor"),
        P("feat"),
    )
    out_specs = P("feat", None, "tensor")
    return jax.shard_map(
        per_device, mesh=mesh, in_specs=in_specs, out_specs=out_specs, check_vma=False
    )
```

profile of v0, /device:TPU:0, one launch (start us, length us, event | category | flops | bytes accessed | tf_op | source)
XLA Modules:
  0.0 378.7 jit_solution(12442276987463202123)
XLA Ops:
  9.9 1.2 reduce-window.6
  11.5 25.1 %scatter_fusion = s32[32,64]{1,0:T(8,128)S(1)} fusion(s32[32,64]{1,0:T(8,128)S(1)} %broadcast_in_dim.77, s32[512]{0:T(512)S(1)} %bitcast.63, s32[512]{0:T(512)S(1)} %get-tuple-element.7), kind=kCustom, calls=%fused_computation.4 | custom fusion | bytes 10240 | tf_op jit(solution)/shard_map/scatter | solution.py:94
  36.6 15.6 %all_to_all.14 = s32[32,1,64]{2,1,0:T(1,128)S(1)} all-to-all(s32[32,1,64]{2,1,0:T(1,128)S(1)} %bitcast.60), channel_id=1, replica_groups=mesh['tensor'=4,'feat'=32] {'feat'}, dimensions={0} | all-to-all | bytes 16384 | tf_op jit(solution)/shard_map/all_to_all | solution.py:96
  52.4 16.4 %gather_fusion = bf16[2048,1152]{1,0:T(8,128)(2,1)} fusion(bf16[4096,1152]{1,0:T(8,128)(2,1)} %param.17, s32[2048]{0:T(1024)S(1)} %broadcast_clamp_fusion), kind=kCustom, calls=%fused_computation | custom fusion | bytes 9445376 | tf_op jit(solution)/shard_map/gather | solution.py:98
  68.8 4.2 %broadcast_select_fusion = bf16[32,64,1152]{2,1,0:T(8,128)(2,1)} fusion(bf16[32,64,1152]{2,1,0:T(8,128)(2,1)} %bitcast.64, pred[32,64]{1,0:T(8,128)(4,1)S(1)} %compare_bitcast_fusion), kind=kLoop, calls=%fused_computation.8 | loop fusion | flops 2359296 | bytes 9439232 | tf_op jit(solution)/shard_map/jit(_where)/select_n | solution.py:97
  73.0 5.0 %all-to-all-start.1 = ((bf16[32,64,1152]{2,1,0:T(8,128)(2,1)}), bf16[32,64,1152]{2,1,0:T(8,128)(2,1)}, u32[]{:S(2)}, u32[]{:S(2)}) async-start(bf16[32,64,1152]{2,1,0:T(8,128)(2,1)} %broadcast_select_fusion), calls=%async_computation.1 | async-start | bytes 9437184 | tf_op jit(solution)/shard_map/all_to_all | solution.py:100
  78.1 11.2 %gather_fusion.2 = bf16[1024,1152]{1,0:T(8,128)(2,1)} fusion(bf16[4096,1152]{1,0:T(8,128)(2,1)} %param.16, s32[1024]{0:T(1024)S(1)} %fusion.7), kind=kCustom, calls=%fused_computation.2 | custom fusion | bytes 4722688 | tf_op jit(solution)/shard_map/gather | solution.py:50
  89.3 3.7 select_convert_fusion
  93.1 46.8 %all-to-all-done.1 = bf16[32,64,1152]{2,1,0:T(8,128)(2,1)} async-done(((bf16[32,64,1152]{2,1,0:T(8,128)(2,1)}), bf16[32,64,1152]{2,1,0:T(8,128)(2,1)}, u32[]{:S(2)}, u32[]{:S(2)}) %all-to-all-start.1) | async-done | bytes 4718624 | tf_op jit(solution)/shard_map/all_to_all | solution.py:100
  139.9 11.0 %gather_fusion.1 = bf16[512,1152]{1,0:T(8,128)(2,1)} fusion(bf16[32,64,1152]{2,1,0:T(8,128)(2,1)} %all-to-all-done.1, s32[512]{0:T(512)S(1)} %bitcast.62), kind=kCustom, calls=%fused_computation.1 | custom fusion | bytes 2363392 | tf_op jit(solution)/shard_map/gather | solution.py:101
  150.9 4.1 %convolution_bitcast_fusion.1 = f32[1024,512]{0,1:T(8,128)} fusion(bf16[1152,1024]{1,0:T(8,128)(2,1)S(1)} %copy-done, bf16[512,1152]{1,0:T(8,128)(2,1)} %gather_fusion.1, f32[1152]{0:T(1024)S(1)} %copy-done.10), kind=kOutput, calls=%fused_computation.13 | convolution fusion | flops 1209729024 | bytes 5640704 | tf_op jit(solution)/shard_map/dot_general | solution.py:105
  155.1 69.4 %all-reduce.2.cloned.1.call-done = bf16[1024,1152]{1,0:T(8,128)(2,1)} async-done(((bf16[1024,1152]{1,0:T(8,128)(2,1)}), bf16[1024,1152]{1,0:T(8,128)(2,1)}) %all-reduce.2.cloned.1.call-update) | async-done | bytes 2359312 | tf_op jit(solution)/shard_map/psum | solution.py:51
  224.5 10.1 %convolution_bitcast_fusion = f32[2048,1024]{0,1:T(8,128)} fusion(bf16[1024,1152]{1,0:T(8,128)(2,1)} %all-reduce.2.cloned.1.call-done, bf16[2048,1152]{1,0:T(8,128)(2,1)} %param.20), kind=kOutput, calls=%fused_computation.9 | convolution fusion | flops 4831838208 | bytes 15466496 | tf_op jit(solution)/shard_map/dot_general | solution.py:54
  235.4 25.6 %all_gather.3 = bf16[512,768]{1,0:T(8,128)(2,1)S(1)} all-gather(bf16[16,768]{1,0:T(8,128)(2,1)S(1)} %pad_maximum_fusion), channel_id=1, replica_groups=mesh['tensor'=4,'feat'=32] {'feat'}, dimensions={0}, use_global_device_ids=true | all-gather | bytes 811008 | tf_op jit(solution)/shard_map/all_gather | solution.py:17
  261.9 4.0 %gather_fusion.3 = bf16[1024,512]{1,0:T(8,128)(2,1)S(1)} fusion(bf16[512,512]{1,0:T(8,128)(2,1)S(1)} %slice.28, s32[1024]{0:T(1024)S(1)} %fusion.8), kind=kCustom, calls=%fused_computation.3 | custom fusion | bytes 2101248 | tf_op jit(solution)/shard_map/gather | solution.py:46
  266.5 4.0 %fusion.17 = (f32[1024,2,2]{0,2,1:T(2,128)S(1)}, f32[1024,2,2,512]{0,3,2,1:T(8,128)S(1)}) fusion(bf16[512,2,128,1]{0,2,3,1:T(8,128)(2,1)} %bitcast.67, bf16[1024,2,2,128]{3,2,1,0:T(2,128)(2,1)S(1)} %reshape.223, pred[1024,512]{0,1:T(8,128)(4,1)S(1)} %iota_compare_fusion), kind=kOutput, calls=%fused_computation.69 | convolution fusion | flops 545255424 | bytes 10240000 | tf_op jit(solution)/shard_map/bkge,tke->bkgt/dot_general | solution.py:66
  271.4 4.6 %fusion.18 = f32[512,1024]{1,0:T(8,128)} fusion(bf16[512,1152]{1,0:T(8,128)(2,1)S(1)} %copy-done.3, bf16[1024,1152]{1,0:T(8,128)(2,1)} %all-reduce.2.cloned.1.call-done), kind=kOutput, calls=%fused_computation.70 | convolution fusion | flops 1207959552 | bytes 5636096 | tf_op jit(solution)/shard_map/dot_general | solution.py:116
  276.0 1.8 convert_element_type.41
  277.7 37.1 %reduce-scatter.6.cloned.1.call-done = f32[512,1024]{0,1:T(8,128)} async-done(((f32[2048,1024]{0,1:T(8,128)}), f32[512,1024]{0,1:T(8,128)}) %reduce-scatter.6.cloned.1.call-update) | async-done | bytes 2097168 | tf_op jit(solution)/shard_map/reduce_scatter | solution.py:53
  314.9 1.7 convert_element_type.42
  316.9 5.3 %convert_bitcast_fusion = bf16[16,1024,2,128]{3,0,2,1:T(8,128)(2,1)} fusion(bf16[2,2,128,1024]{2,1,0,3:T(2,128)(2,1)S(1)} %reshape.221, bf16[1024,2,2,16]{3,2,1,0:T(2,128)(2,1)S(1)} %copy.37), kind=kOutput, calls=%fused_computation.6 | convolution fusion | flops 16777216 | bytes 9568256 | tf_op jit(solution)/shard_map/bkgt,kgeb->tbke/dot_general | solution.py:82
  322.2 12.3 %copy.38 = bf16[16,1024,2,128]{1,3,2,0:T(8,128)(2,1)} copy(bf16[16,1024,2,128]{3,0,2,1:T(8,128)(2,1)} %convert_bitcast_fusion) | data formatting | bytes 16777216 | tf_op jit(solution)/shard_map/convert_element_type | solution.py:83
  334.5 7.1 %add_multiply_fusion = f32[16,32,1024]{2,1,0:T(8,128)} fusion(f32[16,32,1024]{2,1,0:T(8,128)} %bitcast.65, bf16[256,16,32]{0,2,1:T(8,128)(2,1)S(1)} %bitcast.66, bf16[16,1024,256]{1,2,0:T(8,128)(2,1)} %bitcast.61, f32[16]{0:T(128)S(1)} %copy-done.8, f32[16,32]{1,0:T(8,128)S(1)} %copy-done.4, pred[16,1024]{1,0:T(8,128)(4,1)S(1)} %broadcast_compare_fusion), kind=kOutput, calls=%fused_computation.11 | convolution fusion | flops 270532608 | bytes 12863552 | tf_op jit(solution)/shard_map/jtk,tbj->tkb/dot_general | solution.py:113
  341.7 29.4 %reduce-scatter.8.cloned.1.call-done = f32[16,32,256]{2,1,0:T(8,128)} async-done(((f32[16,32,1024]{2,1,0:T(8,128)}), f32[16,32,256]{2,1,0:T(8,128)}) %reduce-scatter.8.cloned.1.call-update) | async-done | bytes 524304 | tf_op jit(solution)/shard_map/reduce_scatter | solution.py:123
  (61 shorter events, 6.6 us)
Async XLA Ops:
  7.4 143.5 %copy-start = (bf16[1152,1024]{1,0:T(8,128)(2,1)S(1)}, bf16[1152,1024]{1,0:T(8,128)(2,1)}, u32[]{:S(2)}) copy-start(bf16[1152,1024]{1,0:T(8,128)(2,1)} %param.21) | copy-start | bytes 7077892
  73.0 5.1 %copy-start.7 = (s32[1024]{0:T(1024)S(1)}, s32[1024]{0:T(1024)}, u32[]{:S(2)}) copy-start(s32[1024]{0:T(1024)} %param.14) | copy-start | bytes 12292
  73.0 66.9 %all-to-all-start.1 = ((bf16[32,64,1152]{2,1,0:T(8,128)(2,1)}), bf16[32,64,1152]{2,1,0:T(8,128)(2,1)}, u32[]{:S(2)}, u32[]{:S(2)}) async-start(bf16[32,64,1152]{2,1,0:T(8,128)(2,1)} %broadcast_select_fusion), calls=%async_computation.1 | async-start | bytes 9437184 | tf_op jit(solution)/shard_map/all_to_all | solution.py:100
  78.0 146.5 %all-reduce.2.cloned.1.call-start = ((), (), s32[]{:S(2)}) async-start(), calls=%async_computation.5 | async-start | bytes 4718592 | tf_op jit(solution)/shard_map/psum | solution.py:51
  93.0 182.9 %reduce-scatter.4.cloned.1.call-start = ((), (), s32[]{:S(2)}) async-start(), calls=%async_computation.6 | async-start | bytes 2621440 | tf_op jit(solution)/shard_map/reduce_scatter | solution.py:104
  139.9 11.0 %copy-start.10 = (f32[1152]{0:T(1024)S(1)}, f32[1152]{0:T(1024)}, u32[]{:S(2)}) copy-start(f32[1152]{0:T(1024)} %param.22) | copy-start | bytes 13828
  155.1 159.8 %reduce-scatter.6.cloned.1.call-start = ((), (), s32[]{:S(2)}) async-start(), calls=%async_computation.7 | async-start | bytes 10485760 | tf_op jit(solution)/shard_map/reduce_scatter | solution.py:53
  234.7 0.7 copy-start.6
  234.7 0.7 copy-start.9
  234.7 27.2 %copy-start.5 = (s32[1024]{0:T(1024)S(1)}, s32[1024]{0:T(1024)}, u32[]{:S(2)}) copy-start(s32[1024]{0:T(1024)} %param.15) | copy-start | bytes 12292
  234.7 136.4 %reduce-scatter.8.cloned.1.call-start = ((), (), s32[]{:S(2)}) async-start(), calls=%async_computation.8 | async-start | bytes 2621440 | tf_op jit(solution)/shard_map/reduce_scatter | solution.py:123
  266.5 4.9 %copy-start.3 = (bf16[512,1152]{1,0:T(8,128)(2,1)S(1)}, bf16[512,1152]{1,0:T(8,128)(2,1)}, u32[]{:S(2)}) copy-start(bf16[512,1152]{1,0:T(8,128)(2,1)} %gather_fusion.1) | copy-start | bytes 3538948
  322.2 12.3 %copy-start.2 = (bf16[256,512]{0,1:T(8,128)(2,1)S(1)}, bf16[256,512]{0,1:T(8,128)(2,1)}, u32[]{:S(2)}) copy-start(bf16[256,512]{0,1:T(8,128)(2,1)} %convert_element_type.41) | copy-start | bytes 786436
  322.2 12.3 %copy-start.4 = (f32[16,32]{1,0:T(8,128)S(1)}, f32[16,32]{1,0:T(8,128)}, u32[]{:S(2)}) copy-start(f32[16,32]{1,0:T(8,128)} %param.13) | copy-start | bytes 6148
  322.2 12.3 %copy-start.8 = (f32[16]{0:T(128)S(1)}, f32[16]{0:T(128)}, u32[]{:S(2)}) copy-start(f32[16]{0:T(128)} %param.23) | copy-start | bytes 196
  334.5 36.6 %copy-start.1 = (bf16[1152,1024]{1,0:T(8,128)(2,1)S(1)}, bf16[1152,1024]{1,0:T(8,128)(2,1)}, u32[]{:S(2)}) copy-start(bf16[1152,1024]{1,0:T(8,128)(2,1)} %param.21) | copy-start | bytes 7077892
Sparse Core Ops, SparseCore 0:
  93.1 131.3 all-reduce.1
Sparse Core Ops, SparseCore 1:
  155.1 30.8 reduce-scatter.3
  234.8 80.0 reduce-scatter.5
  341.7 29.3 reduce-scatter.7
where the time goes:
time: 380 us; the launch traced here: 379 us
  waiting for transfers between devices  183 us (48%)
  local copies, waits for them, and re-layouts  85.8 us (23%)
  blocking collectives  41.2 us (11%)
  matrix products  35.2 us (9%)
  between operations  15.2 us (4%)
  other arithmetic  13.2 us (3%)
  starting transfers between devices  5.16 us (1%)
    psum x1, waiting for transfers between devices, per_device(): seed_row_block = lax.psum(seed_part.astype(jnp.bfloat16), 'feat')  69.4 us
    all_to_all x1, waiting for transfers between devices, per_device(): lax.all_to_all(found_rows, 'feat', split_axis=0, concat_axis=0, tiled=True)  46.8 us
    reduce_scatter x1, waiting for transfers between devices, per_device(): lax.psum_scatter(lax.dot_general(w_piece, seed_row_block, (((1,), (1,)),...  37.1 us
    reduce_scatter x1, waiting for transfers between devices, per_device(): lax.psum_scatter(edge_term, 'tensor', scatter_dimension=2, tiled=True)  29.4 us
    all_gather x1, blocking collectives, side_by_side(): out, at, outs = (lax.all_gather(both, axis, axis=dim, tiled=True), 0, [])  25.6 us
    scatter x1, local copies, waits for them, and re-layouts, per_device(): jnp.full((feat_count, capacity), -1, jnp.int32).at[owner_id, slot_index]  25.1 us
    gather x1, local copies, waits for them, and re-layouts, per_device(): decoder[jnp.maximum(wanted, 0)]  16.4 us
    all_to_all x1, blocking collectives, per_device(): lax.all_to_all(request_table, 'feat', split_axis=0, concat_axis=0, tiled=...  15.6 us
  transfers between devices with their start and end apart: 5, of which 4 were waited for; matrix products, arithmetic and copies ran while one was open for 15% of the time, Pallas kernels for 0%

commit v1 on v0

v1 whole, which is shorter than its diff:
```python
import jax
import jax.numpy as jnp
from jax import lax
from jax.experimental import pallas as pl
from jax.experimental.pallas import tpu as pltpu
from jax.sharding import PartitionSpec as P

HD = 128
H = 16
KVH = 8
NX = 4
NF = 32
MESH = pl.DeviceIdType.MESH
F32 = jnp.float32
BF16 = jnp.bfloat16

softcap_value = 50.0
query_scale = 144.0 ** (-0.5)

VM = pl.BlockSpec(memory_space=pltpu.VMEM)
ANY = pl.BlockSpec(memory_space=pl.ANY)


def nt_dot(a, b):
    return lax.dot_general(a, b, (((1,), (1,)), ((), ())), preferred_element_type=F32)


def nn_dot(a, b):
    return lax.dot_general(a, b, (((1,), (0,)), ((), ())), preferred_element_type=F32)


def feat_id(y, z, c):
    return (y * 4 + z) * 2 + c


def barrier_with(devices):
    barrier = pltpu.get_barrier_semaphore()
    for dev in devices:
        pl.semaphore_signal(barrier, inc=1, device_id=dev, device_id_type=MESH)
    pl.semaphore_wait(barrier, len(devices))


class Copies:
    def __init__(self, send, recv):
        self.send, self.recv, self.all = send, recv, []

    def start(self, src, dst, dev):
        i = len(self.all)
        cp = pltpu.make_async_remote_copy(
            src_ref=src,
            dst_ref=dst,
            send_sem=self.send.at[i],
            recv_sem=self.recv.at[i],
            device_id=dev,
            device_id_type=MESH,
        )
        cp.start()
        self.all.append(cp)
        return cp

    def drain(self):
        for cp in self.all:
            cp.wait_send()


class RingSum:
    def __init__(self, copies, p, plus, minus, block, lo, hi, bufs):
        self.c, self.p, self.plus, self.minus = copies, p, plus, minus
        self.block, self.lo, self.hi = block, lo, hi
        self.lo_in, self.hi_in, self.m_in, self.p_in = bufs

    def at(self, d):
        return self.block((self.p + d) % 4)

    def step1(self):
        far = self.at(2)
        self.a = self.c.start(self.lo(far), self.lo_in, self.plus)
        self.b = self.c.start(self.hi(far), self.hi_in, self.minus)

    def step2(self):
        self.a.wait_recv()
        up = self.lo(self.at(1))
        up[...] = (up[...].astype(F32) + self.lo_in[...].astype(F32)).astype(BF16)
        self.a = self.c.start(self.at(1), self.m_in, self.plus)
        self.b.wait_recv()
        down = self.hi(self.at(3))
        down[...] = (down[...].astype(F32) + self.hi_in[...].astype(F32)).astype(BF16)
        self.b = self.c.start(self.at(3), self.p_in, self.minus)

    def result(self):
        self.a.wait_recv()
        self.b.wait_recv()
        return (
            self.at(0)[...].astype(F32) + self.m_in[...].astype(F32) + self.p_in[...].astype(F32)
        )


class RingGather:
    def __init__(self, copies, p, plus, minus, block, lo, hi):
        self.c, self.p, self.plus, self.minus = copies, p, plus, minus
        self.block, self.lo, self.hi = block, lo, hi

    def at(self, d):
        return self.block((self.p + d) % 4)

    def step1(self):
        own = self.at(0)
        self.a = self.c.start(own, own, self.plus)
        self.b = self.c.start(own, own, self.minus)

    def step2(self):
        self.a.wait_recv()
        left = self.lo(self.at(3))
        self.a = self.c.start(left, left, self.plus)
        self.b.wait_recv()
        right = self.hi(self.at(1))
        self.b = self.c.start(right, right, self.minus)

    def finish(self):
        self.a.wait_recv()
        self.b.wait_recv()


def ids_kernel(ids_ref, out_ref, send, recv):
    f = lax.axis_index("feat")
    barrier = pltpu.get_barrier_semaphore()

    def signal(d, carry):
        pl.semaphore_signal(
            barrier, inc=1, device_id={"feat": (f + d) % NF}, device_id_type=MESH
        )
        return carry

    lax.fori_loop(1, NF, signal, 0)
    out_ref[f] = ids_ref[...]
    pl.semaphore_wait(barrier, NF - 1)

    def copy(d):
        return pltpu.make_async_remote_copy(
            src_ref=ids_ref,
            dst_ref=out_ref.at[f],
            send_sem=send.at[d],
            recv_sem=recv.at[d],
            device_id={"feat": (f + d) % NF},
            device_id_type=MESH,
        )

    def start(d, carry):
        copy(d).start()
        return carry

    def wait(d, carry):
        copy(d).wait()
        return carry

    lax.fori_loop(1, NF, start, 0)
    lax.fori_loop(1, NF, wait, 0)


def gather_ids(ids):
    return pl.pallas_call(
        ids_kernel,
        out_shape=jax.ShapeDtypeStruct((NF, 4, 128), jnp.int32),
        in_specs=[VM],
        out_specs=VM,
        scratch_shapes=[pltpu.SemaphoreType.DMA((NF,)), pltpu.SemaphoreType.DMA((NF,))],
        compiler_params=pltpu.CompilerParams(collective_id=0, has_side_effects=True),
        name="ids",
    )(ids)


def seed_kernel(
    part, qk, wout_hbm, seeds, back, qk_all,
    r0, acc0,
    a_lo, a_hi, a_m, a_p, a_acc, a2_lo, a2_hi, a2_m, a2_p,
    b_lo, b_hi, b_m, b_p, b_acc, b2_lo, b2_hi, b2_m, b2_p,
    wout, bk, k_lo, k_hi, k_m, k_p,
    local, send, recv, qsend, qrecv,
):
    x = lax.axis_index("tensor")
    f = lax.axis_index("feat")
    c = f % 2
    z = (f // 2) % 4
    y = f // 8
    chip = f // 2
    wload = pltpu.make_async_copy(wout_hbm, wout, local.at[0])
    wload.start()
    at = lambda yy, zz, cc: {"feat": feat_id(yy, zz, cc)}
    partner = at(y, z, 1 - c)
    yp, ym = at((y + 1) % 4, z, c), at((y + 3) % 4, z, c)
    zp, zm = at(y, (z + 1) % 4, c), at(y, (z + 3) % 4, c)
    xp, xm = {"tensor": (x + 1) % 4}, {"tensor": (x + 3) % 4}

    barrier = pltpu.get_barrier_semaphore()

    def signal(d, carry):
        pl.semaphore_signal(
            barrier,
            inc=1,
            device_id={"feat": ((chip + d) % 16) * 2 + c},
            device_id_type=MESH,
        )
        return carry

    lax.fori_loop(1, 16, signal, 0)
    for dev in (partner, xp, xm):
        pl.semaphore_signal(barrier, inc=1, device_id=dev, device_id_type=MESH)
    qk_all[chip, c] = qk[...]
    pl.semaphore_wait(barrier, 18)

    cs = Copies(send, recv)
    core0 = cs.start(part.at[:, :, 1 - c], r0, partner)

    def qcopy(d):
        return pltpu.make_async_remote_copy(
            src_ref=qk,
            dst_ref=qk_all.at[chip, c],
            send_sem=qsend.at[d],
            recv_sem=qrecv.at[d],
            device_id={"feat": ((chip + d) % 16) * 2 + c},
            device_id_type=MESH,
        )

    core0.wait_recv()
    for yy in range(4):
        acc0[yy] = part[yy, :, c] + r0[yy]

    CA = pl.ds(0, 640)
    CB = pl.ds(640, 512)
    half0 = lambda r: r.at[pl.ds(0, 2)]
    half1 = lambda r: r.at[pl.ds(2, 2)]
    top = lambda r: r.at[pl.ds(0, 16)]
    bot = lambda r: r.at[pl.ds(16, 16)]
    ra = RingSum(cs, y, yp, ym, lambda q: acc0.at[q, :, :, CA], half0, half1, (a_lo, a_hi, a_m, a_p))
    rb = RingSum(cs, z, zp, zm, lambda q: acc0.at[:, q, :, CB], half0, half1, (b_lo, b_hi, b_m, b_p))
    ra.step1()
    rb.step1()
    ra.step2()
    rb.step2()
    a_acc[...] = ra.result().astype(BF16)
    ra2 = RingSum(cs, z, zp, zm, lambda q: a_acc.at[q], top, bot, (a2_lo, a2_hi, a2_m, a2_p))
    ra2.step1()
    b_acc[...] = rb.result().astype(BF16)
    rb2 = RingSum(cs, y, yp, ym, lambda q: b_acc.at[q], top, bot, (b2_lo, b2_hi, b2_m, b2_p))
    rb2.step1()
    ra2.step2()
    rb2.step2()
    seeds[y, z, c, :, 0:640] = ra2.result().astype(BF16)
    seeds[y, z, c, :, 640:1152] = rb2.result().astype(BF16)

    ga = RingGather(cs, z, zp, zm, lambda q: seeds.at[y, q, c, :, CA], top, bot)
    gb = RingGather(cs, y, yp, ym, lambda q: seeds.at[q, z, c, :, CB], top, bot)
    ga.step1()
    gb.step1()

    def qstart(d, carry):
        qcopy(d).start()
        return carry

    lax.fori_loop(1, 16, qstart, 0)

    wload.wait()
    mine = seeds[y, z, c]
    for n in range(4):
        bk[n] = nt_dot(mine, wout[pl.ds(n * 512, 512), :]).astype(BF16)
    rk = RingSum(cs, x, xp, xm, lambda q: bk.at[q], top, bot, (k_lo, k_hi, k_m, k_p))
    rk.step1()
    ga.step2()
    gb.step2()
    rk.step2()
    ga.finish()
    ga2 = RingGather(cs, y, yp, ym, lambda q: seeds.at[q, :, c, :, CA], half0, half1)
    ga2.step1()
    gb.finish()
    gb2 = RingGather(cs, z, zp, zm, lambda q: seeds.at[:, q, c, :, CB], half0, half1)
    gb2.step1()
    back[y, z, c] = rk.result().astype(BF16)
    KA = pl.ds(0, 256)
    KB = pl.ds(256, 256)
    ha = RingGather(cs, z, zp, zm, lambda q: back.at[y, q, c, :, KA], top, bot)
    hb = RingGather(cs, y, yp, ym, lambda q: back.at[q, z, c, :, KB], top, bot)
    ha.step1()
    hb.step1()

    def qwait(d, carry):
        qcopy(d).wait()
        return carry

    lax.fori_loop(1, 16, qwait, 0)
    qx = cs.start(qk_all.at[:, c], qk_all.at[:, c], partner)

    ga2.step2()
    gb2.step2()
    ha.step2()
    hb.step2()
    ha.finish()
    ha2 = RingGather(cs, y, yp, ym, lambda q: back.at[q, :, c, :, KA], half0, half1)
    ha2.step1()
    hb.finish()
    hb2 = RingGather(cs, z, zp, zm, lambda q: back.at[:, q, c, :, KB], half0, half1)
    hb2.step1()
    ga2.finish()
    gb2.finish()
    sx = cs.start(seeds.at[:, :, c], seeds.at[:, :, c], partner)
    ha2.step2()
    hb2.step2()
    ha2.finish()
    hb2.finish()
    bx = cs.start(back.at[:, :, c], back.at[:, :, c], partner)
    qx.wait_recv()
    sx.wait_recv()
    bx.wait_recv()
    cs.drain()


def seed_call(part, qk, w_out):
    ring = lambda lead: [
        pltpu.VMEM((2, 32, lead), BF16), pltpu.VMEM((2, 32, lead), BF16),
        pltpu.VMEM((4, 32, lead), BF16), pltpu.VMEM((4, 32, lead), BF16),
        pltpu.VMEM((4, 32, lead), BF16),
        pltpu.VMEM((16, lead), BF16), pltpu.VMEM((16, lead), BF16),
        pltpu.VMEM((32, lead), BF16), pltpu.VMEM((32, lead), BF16),
    ]
    return pl.pallas_call(
        seed_kernel,
        out_shape=(
            jax.ShapeDtypeStruct((4, 4, 2, 32, 1152), BF16),
            jax.ShapeDtypeStruct((4, 4, 2, 32, 512), BF16),
            jax.ShapeDtypeStruct((16, 2, 16, 768), BF16),
        ),
        in_specs=[VM, VM, ANY],
        out_specs=(VM, VM, VM),
        scratch_shapes=[
            pltpu.VMEM((4, 4, 32, 1152), BF16), pltpu.VMEM((4, 4, 32, 1152), BF16),
            *ring(640), *ring(512),
            pltpu.VMEM((2048, 1152), BF16), pltpu.VMEM((4, 32, 512), BF16),
            pltpu.VMEM((16, 512), BF16), pltpu.VMEM((16, 512), BF16),
            pltpu.VMEM((32, 512), BF16), pltpu.VMEM((32, 512), BF16),
            pltpu.SemaphoreType.DMA((1,)),
            pltpu.SemaphoreType.DMA((64,)), pltpu.SemaphoreType.DMA((64,)),
            pltpu.SemaphoreType.DMA((16,)), pltpu.SemaphoreType.DMA((16,)),
        ],
        compiler_params=pltpu.CompilerParams(collective_id=1, has_side_effects=True),
        name="seeds",
    )(part, qk, w_out)


def pattern_kernel(qk, pos, out, e_ref):
    f = lax.axis_index("feat")
    tokens = qk.shape[0]
    t = lax.broadcasted_iota(jnp.int32, (tokens, tokens), 0)
    p = lax.broadcasted_iota(jnp.int32, (tokens, tokens), 1)
    causal = t <= p
    pick = (
        lax.broadcasted_iota(jnp.int32, (tokens, pos.shape[1]), 0) == pos[...]
    ).astype(BF16)
    for h in range(4):
        kv = h // 2
        scores = nt_dot(
            qk[:, 512 + kv * HD : 512 + (kv + 1) * HD], qk[:, h * HD : (h + 1) * HD]
        ) * query_scale
        capped = softcap_value * jnp.tanh(scores / softcap_value)
        e = jnp.where(causal, jnp.exp(capped), 0.0)
        e_ref[...] = e
        total = jnp.sum(e, axis=0, keepdims=True)
        own = e_ref[pl.ds(pl.multiple_of(f * 16, 16), 16), :] / total
        head = own.astype(BF16)
        rest = (own - head.astype(F32)).astype(BF16)
        out[h] = nn_dot(head, pick) + nn_dot(rest, pick)


def pattern_call(qk, pos):
    return pl.pallas_call(
        pattern_kernel,
        out_shape=jax.ShapeDtypeStruct((4, 16, 1024), F32),
        in_specs=[VM, VM],
        out_specs=VM,
        scratch_shapes=[pltpu.VMEM((512, 512), F32)],
        name="pattern",
    )(qk, pos)


def tail_kernel(
    recv_hbm, sel, gain, wv, seeds, back, pat, pos, acts, scale, out,
    rows, fetched, projp, proj, direct, edge,
    p_lo, p_hi, p_m, p_p, e_lo, e_hi, e_m, e_p, local, send, recv,
):
    x = lax.axis_index("tensor")
    f = lax.axis_index("feat")
    xp, xm = {"tensor": (x + 1) % 4}, {"tensor": (x + 3) % 4}
    load = pltpu.make_async_copy(recv_hbm, rows, local.at[0])
    load.start()
    barrier_with([xp, xm])
    cs = Copies(send, recv)
    load.wait()

    slots = rows.shape[0]

    def select(i, carry):
        r = pl.ds(pl.multiple_of(i * 128, 128), 128)
        onehot = (
            lax.broadcasted_iota(jnp.int32, (128, slots), 1) == sel[r, :]
        ).astype(BF16)
        got = nn_dot(onehot, rows[...]).astype(BF16)
        fetched[r, :] = got
        gained = (got.astype(F32) * gain[...]).astype(BF16)
        for n in range(4):
            projp[n, r, :] = nn_dot(gained, wv[:, n * 256 : (n + 1) * 256]).astype(BF16)
        return carry

    lax.fori_loop(0, 4, select, 0)
    half0 = lambda r: r.at[pl.ds(0, 256)]
    half1 = lambda r: r.at[pl.ds(256, 256)]
    rp = RingSum(cs, x, xp, xm, lambda q: projp.at[q], half0, half1, (p_lo, p_hi, p_m, p_p))
    rp.step1()

    token = f * 16 + lax.broadcasted_iota(jnp.int32, (512, 256), 0) // 32

    def direct_block(n):
        cols = slice(n * 256, (n + 1) * 256)
        d = nt_dot(fetched[...], seeds[cols, :])
        direct[n] = jnp.where(token == pos[:, cols], d, 0.0)

    direct_block(0)
    direct_block(1)
    rp.step2()
    direct_block(2)
    direct_block(3)
    proj[...] = rp.result().astype(BF16)

    def edge_block(d):
        n = (x + d) % 4
        cols = pl.ds(pl.multiple_of(n * 256, 256), 256)
        for g in range(4):
            r = pl.ds(g * 128, 128)
            acc = jnp.zeros((128, 256), F32)
            for h in range(4):
                kv = h // 2
                mm = nt_dot(
                    proj[r, kv * HD : (kv + 1) * HD], back[cols, h * HD : (h + 1) * HD]
                )
                w = pat[h, pl.ds(g * 4, 4), cols]
                acc = acc + (mm.reshape(4, 32, 256) * w[:, None, :]).reshape(128, 256)
            edge[n, r, :] = (acts[r, :] * (direct[n, r, :] + scale[r, :] * acc)).astype(BF16)

    re = RingSum(cs, x, xp, xm, lambda q: edge.at[q], half0, half1, (e_lo, e_hi, e_m, e_p))
    edge_block(2)
    re.step1()
    edge_block(1)
    edge_block(3)
    re.step2()
    edge_block(0)
    out[...] = re.result()
    cs.drain()


def tail_call(recv, sel, gain, wv, seeds, back, pat, pos, acts, scale):
    half = pltpu.VMEM((256, 256), BF16)
    full = pltpu.VMEM((512, 256), BF16)
    return pl.pallas_call(
        tail_kernel,
        out_shape=jax.ShapeDtypeStruct((512, 256), F32),
        in_specs=[ANY] + [VM] * 9,
        out_specs=VM,
        scratch_shapes=[
            pltpu.VMEM((2048, 1152), BF16), pltpu.VMEM((512, 1152), BF16),
            pltpu.VMEM((4, 512, 256), BF16), full,
            pltpu.VMEM((4, 512, 256), F32), pltpu.VMEM((4, 512, 256), BF16),
            half, half, full, full, half, half, full, full,
            pltpu.SemaphoreType.DMA((1,)),
            pltpu.SemaphoreType.DMA((8,)), pltpu.SemaphoreType.DMA((8,)),
        ],
        compiler_params=pltpu.CompilerParams(collective_id=2, has_side_effects=True),
        name="tail",
    )(recv, sel, gain, wv, seeds, back, pat, pos, acts, scale)


def per_device(
    feat_ids, feat_acts, target_ids, target_token_positions, encoder, decoder,
    queries, keys, w_out, w_value, ln_gain, norm_scale,
):
    f = lax.axis_index("feat")
    feat_dev = encoder.shape[0]
    targets = target_ids.shape[0]
    cap = 64
    ids_all = gather_ids(feat_ids.reshape(4, 128)).reshape(NF, 512)
    owner_all = ids_all // feat_dev
    local_all = ids_all - owner_all * feat_dev
    mine = owner_all == f
    upper = (
        lax.broadcasted_iota(jnp.int32, (512, 512), 0)
        < lax.broadcasted_iota(jnp.int32, (512, 512), 1)
    )
    rank = jnp.dot(mine.astype(BF16), upper.astype(BF16), preferred_element_type=F32)
    key = jnp.where(mine, rank.astype(jnp.int32), -1)
    slots = jnp.arange(cap, dtype=jnp.int32)
    wanted = jnp.sum(
        jnp.where(key[:, None, :] == slots[None, :, None], local_all[:, None, :], 0), axis=2
    )
    found = decoder[wanted.reshape(-1)].reshape(NF, cap, -1)
    returned = lax.all_to_all(found, "feat", split_axis=0, concat_axis=0, tiled=True)

    ids = feat_ids.reshape(512)
    own = ids // feat_dev
    same = (own[:, None] == own[None, :]) & upper.T
    slot = jnp.sum(same.astype(jnp.int32), axis=1)
    sel = (own * cap + slot)[:, None]

    target_owner = target_ids // feat_dev
    target_row = target_ids - target_owner * feat_dev
    is_owner = (target_owner == f)[:, None]
    part = jnp.where(is_owner, encoder[target_row], jnp.zeros((), BF16))
    qk = jnp.concatenate([queries, keys], axis=1)
    seeds, back, qk_all = seed_call(part.reshape(4, 4, 2, 32, -1), qk, w_out)
    pos = target_token_positions[None, :]
    pat = pattern_call(qk_all.reshape(512, 768), pos)
    out = tail_call(
        returned.reshape(NF * cap, -1), sel, ln_gain[None, :], w_value,
        seeds.reshape(targets, -1), back.reshape(targets, -1), pat, pos,
        feat_acts.reshape(512, 1), jnp.repeat(norm_scale, 32)[:, None],
    )
    return out.reshape(16, 32, 256)


def solution(mesh):
    in_specs = (
        P("feat", None),
        P("feat", None),
        P(),
        P(),
        P("feat", "tensor"),
        P("feat", "tensor"),
        P("feat", "tensor"),
        P("feat", "tensor"),
        P(None, "tensor"),
        P("tensor", None),
        P("tensor"),
        P("feat"),
    )
    out_specs = P("feat", None, "tensor")
    return jax.shard_map(
        per_device, mesh=mesh, in_specs=in_specs, out_specs=out_specs, check_vma=False
    )
```

time: 380 us -> 188 us (0.49)
  waiting for transfers between devices: 183 us -> 0.01 us
  Pallas kernels: 0 us -> 142 us
  local copies, waits for them, and re-layouts: 85.8 us -> 33.4 us
  blocking collectives: 41.2 us -> 0 us
  matrix products: 35.2 us -> 1.13 us
  between operations: 15.2 us -> 0.16 us
  other arithmetic: 13.2 us -> 5.15 us
    pallas_call x0 -> x4, Pallas kernels: none -> 142 us  [the longest x1 87.5 us: seed_call(): pl.pallas_call(seed_kernel, out_shape=(jax.ShapeDtypeStruct((4, 4, 2, 32,...]
    psum x1 -> x0, waiting for transfers between devices: 69.4 us -> none  [per_device(): seed_row_block = lax.psum(seed_part.astype(jnp.bfloat16), 'feat')]
    reduce_scatter x3 -> x0, waiting for transfers between devices: 66.6 us -> none  [the longest x1 37.1 us: per_device(): lax.psum_scatter(lax.dot_general(w_piece, seed_row_block, (((1,), (1,)),...]
    all_to_all x1, waiting for transfers between devices: 46.8 us -> 0.01 us  [per_device(): lax.all_to_all(found, 'feat', split_axis=0, concat_axis=0, tiled=True)]
    dot_general x6 -> x1, matrix products: 35.2 us -> 1.13 us  [per_device(): jnp.dot(mine.astype(BF16), upper.astype(BF16), preferred_element_type=F32)]
    all_gather x1 -> x0, blocking collectives: 25.6 us -> none  [side_by_side(): out, at, outs = (lax.all_gather(both, axis, axis=dim, tiled=True), 0, [])]
    scatter x1 -> x0, local copies, waits for them, and re-layouts: 25.1 us -> none  [per_device(): jnp.full((feat_count, capacity), -1, jnp.int32).at[owner_id, slot_index]]
    gather x4 -> x2, local copies, waits for them, and re-layouts: 42.7 us -> 27 us  [the longest x1 16.5 us: per_device(): found = decoder[wanted.reshape(-1)].reshape(NF, cap, -1)]
  transfers between devices with their start and end apart: 5 -> 1, of which waited for: 4 -> 0; matrix products, arithmetic and copies ran while one was open for 15% -> 9% of each run, Pallas kernels for 0% -> 49%
where the time goes in v1:
time: 188 us
  Pallas kernels  142 us (76%)
  local copies, waits for them, and re-layouts  33.4 us (18%)
  starting transfers between devices  5.85 us (3%)
  other arithmetic  5.15 us (3%)
    pallas_call x1, Pallas kernels, seed_call(): pl.pallas_call(seed_kernel, out_shape=(jax.ShapeDtypeStruct((4, 4, 2, 32,...  87.5 us
    pallas_call x1, Pallas kernels, tail_call(): pl.pallas_call(tail_kernel, out_shape=jax.ShapeDtypeStruct((512, 256), F3...  37 us
    gather x1, local copies, waits for them, and re-layouts, per_device(): found = decoder[wanted.reshape(-1)].reshape(NF, cap, -1)  16.5 us
    pallas_call x1, Pallas kernels, gather_ids(): pl.pallas_call(ids_kernel, out_shape=jax.ShapeDtypeStruct((NF, 4, 128), j...  12.8 us
    gather x1, local copies, waits for them, and re-layouts, per_device(): part = jnp.where(is_owner, encoder[target_row], jnp.zeros((), BF16))  10.4 us
    all_to_all x1, starting transfers between devices, per_device(): lax.all_to_all(found, 'feat', split_axis=0, concat_axis=0, tiled=True)  5.85 us
    pallas_call x1, Pallas kernels, pattern_call(): pl.pallas_call(pattern_kernel, out_shape=jax.ShapeDtypeStruct((4, 16, 102...  4.57 us
  transfers between devices with their start and end apart: 1, of which 0 were waited for; matrix products, arithmetic and copies ran while one was open for 9% of the time, Pallas kernels for 49%

profile of v1, /device:TPU:0, one launch (start us, length us, event | category | flops | bytes accessed | tf_op | source)
XLA Modules:
  0.0 187.6 jit_solution(6078403773383432073)
XLA Ops:
  0.0 1.4 reshape.222.ids_ref
  1.4 12.8 %ids.1 = s32[32,4,128]{2,1,0:T(4,128)} custom-call(s32[4,128]{1,0:T(4,128)} %reshape.222.ids_ref), custom_call_target="tpu_custom_call" | custom-call | tf_op jit(solution)/shard_map/ids/pallas_call | solution.py:161
  14.1 0.9 bitcast_subtract_fusion
  15.0 1.1 fusion
  16.2 0.6 select_reduce_fusion
  16.8 0.1 reshape.224
  16.9 16.5 %gather_fusion = bf16[2048,1152]{1,0:T(8,128)(2,1)} fusion(bf16[4096,1152]{1,0:T(8,128)(2,1)} %param.17, s32[2048]{0:T(1024)S(1)} %broadcast_clamp_fusion), kind=kCustom, calls=%fused_computation | custom fusion | bytes 9445376 | tf_op jit(solution)/shard_map/gather | solution.py:500
  33.5 5.9 %all-to-all-start = ((bf16[32,64,1152]{2,1,0:T(8,128)(2,1)}), bf16[32,64,1152]{2,1,0:T(8,128)(2,1)}, u32[]{:S(2)}, u32[]{:S(2)}) async-start(bf16[32,64,1152]{2,1,0:T(8,128)(2,1)} %bitcast.36), calls=%async_computation | async-start | bytes 9437184 | tf_op jit(solution)/shard_map/all_to_all | solution.py:501
  39.3 0.1 reshape.228
  39.4 0.3 reshape.252
  39.7 0.2 convert_reduce_fusion
  39.9 0.2 copy.32
  40.1 0.6 broadcast_in_dim.50.gain
  40.7 0.1 broadcast_in_dim.51
  40.8 0.9 reshape.251.acts
  41.8 1.0 broadcast_in_dim_reshape.4.scale
  42.8 10.4 %gather_fusion.1 = bf16[1024,1152]{1,0:T(8,128)(2,1)S(1)} fusion(bf16[4096,1152]{1,0:T(8,128)(2,1)} %param.16, s32[1024]{0:T(1024)S(1)} %fusion.12), kind=kCustom, calls=%fused_computation.1 | custom fusion | bytes 4722688 | tf_op jit(solution)/shard_map/gather | solution.py:512
  53.3 0.6 pad_maximum_fusion.qk
  53.9 1.9 broadcast_select_fusion.part
  55.7 87.5 %seeds.1 = (bf16[4,4,2,32,1152]{4,3,2,1,0:T(8,128)(2,1)}, bf16[4,4,2,32,512]{4,3,2,1,0:T(8,128)(2,1)}, bf16[16,2,16,768]{3,2,1,0:T(8,128)(2,1)}) custom-call(bf16[4,4,2,32,1152]{4,3,2,1,0:T(8,128)(2,1)} %broadcast_select_fusion.part, bf16[16,768]{1,0:T(8,128)(2,1)} %pad_maximum_fusion.qk, bf16[2048,1152]{1,0:T(8,128)(2,1)} %wout_hbm.1), custom_call_target="tpu_custom_call" | custom-call | tf_op jit(solution)/shard_map/seeds/pallas_call | solution.py:324
  143.2 4.6 %pattern.1.pat = f32[4,16,1024]{2,1,0:T(8,128)} custom-call(bf16[512,768]{1,0:T(8,128)(2,1)} %bitcast.41, s32[1,1024]{1,0:T(1,128)} %bitcast.45), custom_call_target="tpu_custom_call" | custom-call | tf_op jit(solution)/shard_map/pattern/pallas_call | solution.py:373
  147.8 0.9 fusion.4.sel
  148.7 37.0 %tail.1 = f32[512,256]{1,0:T(8,128)} custom-call(bf16[2048,1152]{1,0:T(8,128)(2,1)} %bitcast.2.recv_hbm, s32[512,1]{1,0:T(8,128)} %fusion.4.sel, f32[1,1152]{1,0:T(1,128)} %broadcast_in_dim.50.gain, bf16[1152,1024]{1,0:T(8,128)(2,1)} %wv.1, bf16[1024,1152]{1,0:T(8,128)(2,1)} %bitcast.38, bf16[1024,512]{1,0:T(8,128)(2,1)} %bitcast.40, ...), custom_call_target="tpu_custom_call" | custom-call | tf_op jit(solution)/shard_map/tail/pallas_call | solution.py:460
  185.7 1.9 %copy.47 = f32[16,32,256]{2,1,0:T(8,128)} copy(f32[16,32,256]{2,1,0:T(8,128)} %bitcast.39) | data formatting | bytes 1048576
  (21 shorter events, 0.2 us)
Async XLA Ops:
  33.4 5.9 %copy-start = (s32[16,32]{1,0:T(8,128)S(1)}, s32[16,32]{1,0:T(8,128)}, u32[]{:S(2)}) copy-start(s32[16,32]{1,0:T(8,128)} %param.12) | copy-start | bytes 6148
  33.4 6.7 %copy-start.4 = (f32[1152]{0:T(1024)S(1)}, f32[1152]{0:T(1024)}, u32[]{:S(2)}) copy-start(f32[1152]{0:T(1024)} %param.22) | copy-start | bytes 13828
  33.4 7.3 %copy-start.2 = (s32[1024]{0:T(1024)S(1)}, s32[1024]{0:T(1024)}, u32[]{:S(2)}) copy-start(s32[1024]{0:T(1024)} %param.14) | copy-start | bytes 12292
  33.4 7.4 %copy-start.3 = (f32[16,32]{1,0:T(8,128)S(1)}, f32[16,32]{1,0:T(8,128)}, u32[]{:S(2)}) copy-start(f32[16,32]{1,0:T(8,128)} %param.13) | copy-start | bytes 6148
  33.5 8.3 %copy-start.6 = (f32[16]{0:T(128)S(1)}, f32[16]{0:T(128)}, u32[]{:S(2)}) copy-start(f32[16]{0:T(128)} %param.23) | copy-start | bytes 196
  33.5 115.2 %all-to-all-start = ((bf16[32,64,1152]{2,1,0:T(8,128)(2,1)}), bf16[32,64,1152]{2,1,0:T(8,128)(2,1)}, u32[]{:S(2)}, u32[]{:S(2)}) async-start(bf16[32,64,1152]{2,1,0:T(8,128)(2,1)} %bitcast.36), calls=%async_computation | async-start | bytes 9437184 | tf_op jit(solution)/shard_map/all_to_all | solution.py:501
  42.8 10.4 %copy-start.1 = (bf16[16,512]{1,0:T(8,128)(2,1)S(1)}, bf16[16,512]{1,0:T(8,128)(2,1)}, u32[]{:S(2)}) copy-start(bf16[16,512]{1,0:T(8,128)(2,1)} %param.18) | copy-start | bytes 49156
  42.8 10.4 %copy-start.5 = (bf16[16,256]{1,0:T(8,128)(2,1)S(1)}, bf16[16,256]{1,0:T(8,128)(2,1)}, u32[]{:S(2)}) copy-start(bf16[16,256]{1,0:T(8,128)(2,1)} %param.19) | copy-start | bytes 24580
